TPU v7x, 256 devices: a whole 4x4x8 slice. The times are simulated.
256 devices in a mesh: occa: 8 (over x, core), occb: 4 (over z_lo), rows: 8 (over z_hi, y).
Axes of the slice: x: 4, y: 4, z: 8 (z_hi: 2, z_lo: 4; z = z_hi * 4 + z_lo), core: 2. Of those that a mesh axis runs over, the one named last changes fastest.
Arguments:
- density: float32 [512, 8, 4, 2, 512], P('rows', 'occa', 'occb'), may hold values from -6 to 6
- operators: float32 [5, 512, 512], P(None, 'rows'), as said below
- rates: float32 [2], replicated, may hold values from 0.05 to 0.5
- coupling: float32 [2, 2], replicated, may hold values from 0.3 to 1
- keep_mask: int32 [8, 4], P('occa', 'occb'), may hold values 0 or 1
Outputs:
- advanced: float32 [512, 8, 4, 2, 512], P('rows', 'occa', 'occb')
Inputs may be any that keep to these rules, and one draw needn't show every extreme that they name: `keep_mask`: 1 keeps an auxiliary matrix in the hierarchy, 0 removes it. `operators`: each of the five matrices is symmetric.
All inputs are finite; a program needn't handle non-finite values. No bound on the sum of `keep_mask` on one device may be relied on, other than what follows from the above.
Results may differ from a plain program's by a relative error of at most 0.00005.
Values sent between devices are 32-bit elements; how exact they have to be, the bound alone decides.
A program may use at most 64 MiB of HBM per device.

v0:
```python
import jax
import jax.numpy as jnp
from jax import lax
from jax.sharding import PartitionSpec as P

TIME_STEP = 0.05
PRECISE = lax.Precision.HIGHEST


def padded(cells, sides, width):
    for axis, dim in sides:
        count = lax.axis_size(axis)
        ends = count - 1
        head = lax.slice_in_dim(cells, 0, width, axis=dim)
        tail = lax.slice_in_dim(cells, cells.shape[dim] - width, cells.shape[dim], axis=dim)
        cells = jnp.concatenate(
            [
                lax.ppermute(tail, axis, [(i, (i + 1) % count) for i in range(ends)]),
                cells,
                lax.ppermute(head, axis, [((i + 1) % count, i) for i in range(ends)]),
            ],
            axis=dim,
        )
    return cells


def neighbours(extended, count_a, count_b):
    return jnp.stack(
        [
            extended[:, 1 : count_a + 1, 1 : count_b + 1],
            extended[:, 2 : count_a + 2, 1 : count_b + 1],
            extended[:, 0:count_a, 1 : count_b + 1],
            extended[:, 1 : count_a + 1, 2 : count_b + 2],
            extended[:, 1 : count_a + 1, 0:count_b],
        ],
        axis=3,
    )


def ladder_factors(occ_a, occ_b, coupling):
    zeros = jnp.zeros_like(occ_a + occ_b)
    up_a = jnp.sqrt(occ_a + 1.0)
    up_b = jnp.sqrt(occ_b + 1.0)
    down_a = jnp.sqrt(occ_a)
    down_b = jnp.sqrt(occ_b)
    factor_re = jnp.stack(
        [zeros, zeros, down_a * coupling[0, 1], zeros, down_b * coupling[1, 1]], axis=-1
    )
    factor_im = jnp.stack(
        [zeros - 1.0, -up_a, -down_a * coupling[0, 0], -up_b, -down_b * coupling[1, 0]], axis=-1
    )
    return (factor_re, factor_im)


def weighted(stacked, factor_re, factor_im):
    part_re = stacked[..., 0, :]
    part_im = stacked[..., 1, :]
    scale_re = factor_re[None, :, :, :, None]
    scale_im = factor_im[None, :, :, :, None]
    return jnp.stack(
        [scale_re * part_re - scale_im * part_im, scale_re * part_im + scale_im * part_re], axis=4
    )


def shards(density, operators, rates, coupling, keep_mask):
    row_count = density.shape[0]
    count_a = density.shape[1]
    count_b = density.shape[2]
    full_ops = lax.all_gather(operators, "rows", axis=1, tiled=True)
    occ_a = (lax.axis_index("occa") * count_a + jnp.arange(count_a)).astype(jnp.float32)[:, None]
    occ_b = (lax.axis_index("occb") * count_b + jnp.arange(count_b)).astype(jnp.float32)[None, :]
    row_start = lax.axis_index("rows") * row_count
    factor_re, factor_im = ladder_factors(occ_a, occ_b, coupling)
    damping = (occ_a * rates[0] + occ_b * rates[1])[None, :, :, None, None]
    kept = keep_mask.astype(jnp.float32)[None, :, :, None, None]

    def derivative(field):
        extended = padded(field, (("occa", 1), ("occb", 2)), 1)
        stacked = neighbours(extended, count_a, count_b)
        right_ops = weighted(stacked, factor_re, -factor_im)
        right_part = jnp.einsum("iabkpc,kcm->iabpm", right_ops, full_ops, precision=PRECISE)
        left_ops = weighted(stacked, factor_re, factor_im)
        op_slice = lax.dynamic_slice_in_dim(full_ops, row_start, row_count, 2)
        left_part = lax.psum_scatter(
            jnp.einsum("kic,cabkpm->iabpm", op_slice, left_ops, precision=PRECISE),
            "rows",
            scatter_dimension=0,
            tiled=True,
        )
        return (left_part + right_part - damping * field) * kept

    start = density * kept
    first = derivative(start)
    second = derivative(first)
    return start + TIME_STEP * first + 0.5 * TIME_STEP * TIME_STEP * second


def solution(mesh):
    placed = (
        P("rows", "occa", "occb", None, None),
        P(None, "rows", None),
        P(),
        P(),
        P("occa", "occb"),
    )
    return jax.shard_map(
        shards,
        mesh=mesh,
        in_specs=placed,
        out_specs=P("rows", "occa", "occb", None, None),
        check_vma=False,
    )
```

profile of v0, /device:TPU:2, one launch (start us, length us, event | category | flops | bytes accessed | tf_op | source)
XLA Modules:
  0.0 391.8 jit_solution(12021623194083770563)
XLA Ops:
  6.5 0.0 all-gather.2.cloned.1.call-start
  6.5 0.7 all-gather.2.cloned.1.call-update
  7.3 0.0 copy-start.1
  7.3 0.0 reduce-scatter.3.cloned.1.call-start
  8.0 1.0 bitcast_dynamic-update-slice_fusion.5
  9.0 1.9 collective-permute-start.1
  10.9 3.6 collective-permute-start
  14.6 2.1 collective-permute-done.1
  16.7 1.8 collective-permute-done
  18.4 0.1 pad_maximum_fusion
  18.5 1.3 collective-permute-start.2
  20.0 0.0 copy-done.1
  20.0 0.7 fusion.59
  23.2 0.1 stack.103
  23.3 0.1 stack.99
  23.4 4.6 %collective-permute-start.3 = (f32[64,3,1,2,512]{4,0,3,2,1:T(8,128)S(1)}, f32[64,3,1,2,512]{4,0,3,2,1:T(8,128)S(1)}, u32[]{:S(2)}, u32[]{:S(2)}) collective-permute-start(f32[64,3,1,2,512]{4,0,3,2,1:T(8,128)S(1)} %pad_maximum_fusion), channel_id=1, source_target_pairs={{0,8},{8,16},{16,24},{1,9},{9,17},{17,25},{2,10},{10,18},{18,26},{... | collective-permute-start | bytes 2359304 | tf_op jit(solution)/shard_map/ppermute | solution.py:18
  28.0 0.1 fusion.52
  28.1 25.9 %collective-permute-done.2 = f32[64,3,1,2,512]{4,0,3,2,1:T(8,128)} collective-permute-done((f32[64,3,1,2,512]{4,0,3,2,1:T(8,128)S(1)}, f32[64,3,1,2,512]{4,0,3,2,1:T(8,128)}, u32[]{:S(2)}, u32[]{:S(2)}) %collective-permute-start.2) | collective-permute-done | bytes 786464 | tf_op jit(solution)/shard_map/ppermute | solution.py:20
  54.0 1.0 fusion.49
  54.9 2.4 collective-permute-done.3
  57.4 0.0 copy-start
  57.4 1.1 copy-done
  58.5 1.8 multiply_subtract_fusion.2
  60.3 82.9 %all-gather.2.cloned.1.call-done = f32[5,512,512]{2,1,0:T(8,128)} async-done(((f32[5,64,512]{2,1,0:T(8,128)}), f32[5,512,512]{2,1,0:T(8,128)}) %all-gather.2.cloned.1.call-update) | async-done | bytes 5242896 | tf_op jit(solution)/shard_map/all_gather | solution.py:69
  143.2 6.4 %convolution_bitcast_fusion.1 = f32[512,1,1,2,512]{4,0,3,2,1:T(8,128)} fusion(f32[64,1,1,5,1,512]{5,0,3,4,2,1:T(8,128)S(1)} %get-tuple-element.17, f32[64,1,1,5,1,512]{5,0,3,4,2,1:T(8,128)S(1)} %get-tuple-element.18, f32[5,512,512]{2,1,0:T(8,128)} %all-gather.2.cloned.1.call-done, s32[]{:T(128)S(6)} %select_n.4), kind=kOutput, calls=%fused_computation.5 | convolution fusion | flops 2013593600 | bytes 4718596 | tf_op jit(solution)/shard_map/kic,cabkpm->iabpm/dot_general | solution.py:85
  149.6 0.0 copy-start.2
  149.6 0.0 reduce-scatter.3.cloned.1.call-update
  149.6 0.0 reduce-scatter.5.cloned.1.call-start
  149.7 0.6 copy-done.2
  150.3 0.6 fusion.60
  152.1 88.1 %reduce-scatter.3.cloned.1.call-done = f32[64,1,1,2,512]{4,0,3,2,1:T(8,128)} async-done(((f32[512,1,1,2,512]{4,0,3,2,1:T(8,128)}), f32[64,1,1,2,512]{4,0,3,2,1:T(8,128)}) %reduce-scatter.3.cloned.1.call-update) | async-done | bytes 262160 | tf_op jit(solution)/shard_map/reduce_scatter | solution.py:84
  240.2 5.5 %bitcast_dynamic-update-slice_fusion.2 = (f32[64,1,1,5,2,512]{5,0,3,4,2,1:T(8,128)S(1)}, f32[64,1,1,2,512]{4,0,3,2,1:T(8,128)S(1)}) fusion(f32[]{:T(128)} %bitcast, f32[64,1,1,2,512]{4,0,3,2,1:T(8,128)S(1)} %get-tuple-element.6, f32[]{:T(128)} %bitcast.30, f32[64,1,1,2,512]{4,0,3,2,1:T(8,128)} %reduce-scatter.3.cloned.1.call-done, ...), kind=kOutput, calls=%fused_computation.54 | convolution fusion | flops 2013855744 | bytes 7602184 | tf_op jit(solution)/shard_map/iabkpc,kcm->iabpm/dot_general | solution.py:81
  245.7 1.9 collective-permute-start.5
  247.6 3.6 collective-permute-start.4
  251.3 2.1 collective-permute-done.5
  253.4 1.8 collective-permute-done.4
  255.2 0.1 pad_maximum_fusion.1
  255.2 1.3 collective-permute-start.6
  256.5 4.8 %collective-permute-start.7 = (f32[64,3,1,2,512]{4,0,3,2,1:T(8,128)S(1)}, f32[64,3,1,2,512]{4,0,3,2,1:T(8,128)S(1)}, u32[]{:S(2)}, u32[]{:S(2)}) collective-permute-start(f32[64,3,1,2,512]{4,0,3,2,1:T(8,128)S(1)} %pad_maximum_fusion.1), channel_id=1, source_target_pairs={{0,8},{8,16},{16,24},{1,9},{9,17},{17,25},{2,10},{10,18},{18,26},{... | collective-permute-start | bytes 2359304 | tf_op jit(solution)/shard_map/ppermute | solution.py:18
  261.4 15.4 %collective-permute-done.6 = f32[64,3,1,2,512]{4,0,3,2,1:T(8,128)S(1)} collective-permute-done((f32[64,3,1,2,512]{4,0,3,2,1:T(8,128)S(1)}, f32[64,3,1,2,512]{4,0,3,2,1:T(8,128)S(1)}, u32[]{:S(2)}, u32[]{:S(2)}) %collective-permute-start.6) | collective-permute-done | bytes 786464 | tf_op jit(solution)/shard_map/ppermute | solution.py:20
  276.8 1.8 collective-permute-done.7
  278.6 0.3 multiply_subtract_fusion
  278.9 6.4 %convolution_bitcast_fusion = f32[512,1,1,2,512]{4,0,3,2,1:T(8,128)} fusion(f32[64,1,1,5,1,512]{5,0,3,4,2,1:T(8,128)S(1)} %get-tuple-element.15, f32[64,1,1,5,1,512]{5,0,3,4,2,1:T(8,128)S(1)} %get-tuple-element.16, f32[5,512,512]{2,1,0:T(8,128)} %all-gather.2.cloned.1.call-done, s32[]{:T(128)S(6)} %select_n.4), kind=kOutput, calls=%fused_computation.4 | convolution fusion | flops 2013593600 | bytes 4718596 | tf_op jit(solution)/shard_map/kic,cabkpm->iabpm/dot_general | solution.py:85
  285.3 0.0 reduce-scatter.5.cloned.1.call-update
  285.3 93.4 %reduce-scatter.5.cloned.1.call-done = f32[64,1,1,2,512]{4,0,3,2,1:T(8,128)} async-done(((f32[512,1,1,2,512]{4,0,3,2,1:T(8,128)}), f32[64,1,1,2,512]{4,0,3,2,1:T(8,128)}) %reduce-scatter.5.cloned.1.call-update) | async-done | bytes 262160 | tf_op jit(solution)/shard_map/reduce_scatter | solution.py:84
  378.8 5.5 %fusion.34 = f32[64,1,1,2,512]{4,0,3,2,1:T(8,128)S(1)} fusion(f32[64,1,1,2,512]{4,0,3,2,1:T(8,128)} %reduce-scatter.5.cloned.1.call-done, f32[5,512,512]{2,1,0:T(8,128)} %all-gather.2.cloned.1.call-done, f32[64,1,1,5,1,512]{5,0,3,4,2,1:T(8,128)S(1)} %get-tuple-element.8, f32[64,1,1,5,1,512]{5,0,3,4,2,1:T(8,128)S(1)} %get-tuple-element.7, ...), kind=kOutput, calls=%fused_computation.28 | convolution fusion | flops 2014117888 | bytes 7602184 | tf_op jit(solution)/shard_map/iabkpc,kcm->iabpm/dot_general | solution.py:81
  384.3 0.9 copy.25
  (9 shorter events, 0.1 us)
Async XLA Ops:
  6.5 136.7 %all-gather.2.cloned.1.call-start = ((), (), s32[]{:S(2)}) async-start(), calls=%async_computation.2 | async-start | bytes 5898240 | tf_op jit(solution)/shard_map/all_gather | solution.py:69
  7.3 12.7 %copy-start.1 = (f32[2,2]{1,0:T(2,128)S(1)}, f32[2,2]{1,0:T(2,128)}, u32[]{:S(2)}) copy-start(f32[2,2]{1,0:T(2,128)} %param.8) | copy-start | bytes 52
  7.3 232.9 %reduce-scatter.3.cloned.1.call-start = ((), (), s32[]{:S(2)}) async-start(), calls=%async_computation.3 | async-start | bytes 2359296 | tf_op jit(solution)/shard_map/reduce_scatter | solution.py:84
  9.0 7.7 %collective-permute-start.1 = (f32[64,1,1,2,512]{4,0,3,2,1:T(8,128)S(1)}, f32[64,1,1,2,512]{4,0,3,2,1:T(8,128)S(1)}, u32[]{:S(2)}, u32[]{:S(2)}) collective-permute-start(f32[64,1,1,2,512]{4,0,3,2,1:T(8,128)S(1)} %get-tuple-element.6), channel_id=1, source_target_pairs={{0,32},{32,64},{64,96},{96,128},{128,160},{160,192},{192,224},{1,3... | collective-permute-start | bytes 786440 | tf_op jit(solution)/shard_map/ppermute | solution.py:18
  10.9 7.5 %collective-permute-start = (f32[64,1,1,2,512]{4,0,3,2,1:T(8,128)S(1)}, f32[64,1,1,2,512]{4,0,3,2,1:T(8,128)S(1)}, u32[]{:S(2)}, u32[]{:S(2)}) collective-permute-start(f32[64,1,1,2,512]{4,0,3,2,1:T(8,128)S(1)} %get-tuple-element.6), channel_id=1, source_target_pairs={{32,0},{64,32},{96,64},{128,96},{160,128},{192,160},{224,192},{33,... | collective-permute-start | bytes 786440 | tf_op jit(solution)/shard_map/ppermute | solution.py:20
  18.5 35.5 %collective-permute-start.2 = (f32[64,3,1,2,512]{4,0,3,2,1:T(8,128)S(1)}, f32[64,3,1,2,512]{4,0,3,2,1:T(8,128)}, u32[]{:S(2)}, u32[]{:S(2)}) collective-permute-start(f32[64,3,1,2,512]{4,0,3,2,1:T(8,128)S(1)} %pad_maximum_fusion), channel_id=1, source_target_pairs={{8,0},{16,8},{24,16},{9,1},{17,9},{25,17},{10,2},{18,10},{26,18},{... | collective-permute-start | bytes 2359304 | tf_op jit(solution)/shard_map/ppermute | solution.py:20
  23.4 34.0 %collective-permute-start.3 = (f32[64,3,1,2,512]{4,0,3,2,1:T(8,128)S(1)}, f32[64,3,1,2,512]{4,0,3,2,1:T(8,128)S(1)}, u32[]{:S(2)}, u32[]{:S(2)}) collective-permute-start(f32[64,3,1,2,512]{4,0,3,2,1:T(8,128)S(1)} %pad_maximum_fusion), channel_id=1, source_target_pairs={{0,8},{8,16},{16,24},{1,9},{9,17},{17,25},{2,10},{10,18},{18,26},{... | collective-permute-start | bytes 2359304 | tf_op jit(solution)/shard_map/ppermute | solution.py:18
  57.4 1.1 copy-start
  149.6 0.7 copy-start.2
  149.6 229.1 %reduce-scatter.5.cloned.1.call-start = ((), (), s32[]{:S(2)}) async-start(), calls=%async_computation.4 | async-start | bytes 2359296 | tf_op jit(solution)/shard_map/reduce_scatter | solution.py:84
  245.7 7.7 %collective-permute-start.5 = (f32[64,1,1,2,512]{4,0,3,2,1:T(8,128)S(1)}, f32[64,1,1,2,512]{4,0,3,2,1:T(8,128)S(1)}, u32[]{:S(2)}, u32[]{:S(2)}) collective-permute-start(f32[64,1,1,2,512]{4,0,3,2,1:T(8,128)S(1)} %get-tuple-element.26), channel_id=1, source_target_pairs={{0,32},{32,64},{64,96},{96,128},{128,160},{160,192},{192,224},{1,3... | collective-permute-start | bytes 786440 | tf_op jit(solution)/shard_map/ppermute | solution.py:18
  247.6 7.5 %collective-permute-start.4 = (f32[64,1,1,2,512]{4,0,3,2,1:T(8,128)S(1)}, f32[64,1,1,2,512]{4,0,3,2,1:T(8,128)S(1)}, u32[]{:S(2)}, u32[]{:S(2)}) collective-permute-start(f32[64,1,1,2,512]{4,0,3,2,1:T(8,128)S(1)} %get-tuple-element.26), channel_id=1, source_target_pairs={{32,0},{64,32},{96,64},{128,96},{160,128},{192,160},{224,192},{33,... | collective-permute-start | bytes 786440 | tf_op jit(solution)/shard_map/ppermute | solution.py:20
  255.2 21.5 %collective-permute-start.6 = (f32[64,3,1,2,512]{4,0,3,2,1:T(8,128)S(1)}, f32[64,3,1,2,512]{4,0,3,2,1:T(8,128)S(1)}, u32[]{:S(2)}, u32[]{:S(2)}) collective-permute-start(f32[64,3,1,2,512]{4,0,3,2,1:T(8,128)S(1)} %pad_maximum_fusion.1), channel_id=1, source_target_pairs={{8,0},{16,8},{24,16},{9,1},{17,9},{25,17},{10,2},{18,10},{26,18},{... | collective-permute-start | bytes 2359304 | tf_op jit(solution)/shard_map/ppermute | solution.py:20
  256.5 22.0 %collective-permute-start.7 = (f32[64,3,1,2,512]{4,0,3,2,1:T(8,128)S(1)}, f32[64,3,1,2,512]{4,0,3,2,1:T(8,128)S(1)}, u32[]{:S(2)}, u32[]{:S(2)}) collective-permute-start(f32[64,3,1,2,512]{4,0,3,2,1:T(8,128)S(1)} %pad_maximum_fusion.1), channel_id=1, source_target_pairs={{0,8},{8,16},{16,24},{1,9},{9,17},{17,25},{2,10},{10,18},{18,26},{... | collective-permute-start | bytes 2359304 | tf_op jit(solution)/shard_map/ppermute | solution.py:18
Sparse Core Ops, SparseCore 0:
  10.0 133.1 all-gather.1
  149.8 90.3 reduce-scatter.2
  285.5 93.2 reduce-scatter.4
where the time goes:
time: 392 us
  waiting for transfers between devices  318 us (81%)
  matrix products  23.9 us (6%)
  starting transfers between devices  23.2 us (6%)
  between operations  17.8 us (5%)
  local copies, waits for them, and re-layouts  5.2 us (1%)
    reduce_scatter x2, waiting for transfers between devices, derivative(): lax.psum_scatter(jnp.einsum('kic,cabkpm->iabpm', op_slice, left_ops, prec...  181 us
    all_gather x1, waiting for transfers between devices, shards(): full_ops = lax.all_gather(operators, 'rows', axis=1, tiled=True)  82.9 us
    ppermute x4, waiting for transfers between devices, padded(): lax.ppermute(head, axis, [((i + 1) % count, i) for i in range(ends)])  44.8 us
    ppermute x4, starting transfers between devices, padded(): lax.ppermute(tail, axis, [(i, (i + 1) % count) for i in range(ends)])  13.2 us
    dot_general x2, matrix products, derivative(): jnp.einsum('kic,cabkpm->iabpm', op_slice, left_ops, precision=PRECISE)  12.8 us
    dot_general x2, matrix products, derivative(): jnp.einsum('iabkpc,kcm->iabpm', right_ops, full_ops, precision=PRECISE)  11.1 us
    ppermute x4, starting transfers between devices, padded(): lax.ppermute(head, axis, [((i + 1) % count, i) for i in range(ends)])  9.87 us
    ppermute x4, waiting for transfers between devices, padded(): lax.ppermute(tail, axis, [(i, (i + 1) % count) for i in range(ends)])  8.42 us
  transfers between devices with their start and end apart: 11, of which 11 were waited for; matrix products, arithmetic and copies ran while one was open for 1% of the time, Pallas kernels for 0%

commit v1 on v0

--- a/solution.py
+++ b/solution.py
@@ -2,6 +2,7 @@
 import jax.numpy as jnp
 from jax import lax
 from jax.sharding import PartitionSpec as P
+from jax.lax import all_to_all, axis_size
 
 TIME_STEP = 0.05
 PRECISE = lax.Precision.HIGHEST
@@ -66,7 +67,9 @@
     row_count = density.shape[0]
     count_a = density.shape[1]
     count_b = density.shape[2]
-    full_ops = lax.all_gather(operators, "rows", axis=1, tiled=True)
+    full_ops = jnp.concatenate(
+        all_to_all(jnp.stack([operators] * axis_size("rows"), axis=0), "rows", 0, 0), axis=1
+    )
     occ_a = (lax.axis_index("occa") * count_a + jnp.arange(count_a)).astype(jnp.float32)[:, None]
     occ_b = (lax.axis_index("occb") * count_b + jnp.arange(count_b)).astype(jnp.float32)[None, :]
     row_start = lax.axis_index("rows") * row_count

time: 392 us -> 417 us (1.064)
  starting transfers between devices: 23.2 us -> 34.4 us
  local copies, waits for them, and re-layouts: 5.2 us -> 14.7 us
  waiting for transfers between devices: 318 us -> 324 us
    ppermute x4, waiting for transfers between devices: 44.8 us -> 130 us  [padded(): lax.ppermute(head, axis, [((i + 1) % count, i) for i in range(ends)])]
    all_gather x1 -> x0, waiting for transfers between devices: 82.9 us -> none  [shards(): full_ops = lax.all_gather(operators, 'rows', axis=1, tiled=True)]
    all_to_all x0 -> x1, starting transfers between devices: none -> 11.2 us  [shards(): all_to_all(jnp.stack([operators] * axis_size('rows'), axis=0), 'rows', 0, 0)]
    reduce_scatter x2, waiting for transfers between devices: 181 us -> 188 us  [derivative(): lax.psum_scatter(jnp.einsum('kic,cabkpm->iabpm', op_slice, left_ops, prec...]
  transfers between devices with their start and end apart: 11 -> 11, of which waited for: 11 -> 9; matrix products, arithmetic and copies ran while one was open for 1% -> 1% of each run, Pallas kernels for 0% -> 0%
where the time goes in v1:
time: 417 us
  waiting for transfers between devices  324 us (78%)
  starting transfers between devices  34.4 us (8%)
  matrix products  22.6 us (5%)
  between operations  18.4 us (4%)
  local copies, waits for them, and re-layouts  14.7 us (4%)
    reduce_scatter x2, waiting for transfers between devices, derivative(): lax.psum_scatter(jnp.einsum('kic,cabkpm->iabpm', op_slice, left_ops, prec...  188 us
    ppermute x4, waiting for transfers between devices, padded(): lax.ppermute(head, axis, [((i + 1) % count, i) for i in range(ends)])  130 us
    ppermute x4, starting transfers between devices, padded(): lax.ppermute(tail, axis, [(i, (i + 1) % count) for i in range(ends)])  13.2 us
    dot_general x2, matrix products, derivative(): jnp.einsum('kic,cabkpm->iabpm', op_slice, left_ops, precision=PRECISE)  11.5 us
    all_to_all x1, starting transfers between devices, shards(): all_to_all(jnp.stack([operators] * axis_size('rows'), axis=0), 'rows', 0, 0)  11.2 us
    dot_general x2, matrix products, derivative(): jnp.einsum('iabkpc,kcm->iabpm', right_ops, full_ops, precision=PRECISE)  11.1 us
    ppermute x4, starting transfers between devices, padded(): lax.ppermute(head, axis, [((i + 1) % count, i) for i in range(ends)])  9.87 us
  transfers between devices with their start and end apart: 11, of which 9 were waited for; matrix products, arithmetic and copies ran while one was open for 1% of the time, Pallas kernels for 0%

profile of v1, /device:TPU:2, one launch (start us, length us, event | category | flops | bytes accessed | tf_op | source)
XLA Modules:
  0.0 416.8 jit_solution(2988087051463981139)
XLA Ops:
  6.5 4.1 stack.97
  10.7 11.2 %all-to-all-start = ((f32[8,5,64,512]{3,2,1,0:T(8,128)}), f32[8,5,64,512]{3,2,1,0:T(8,128)}, u32[]{:S(2)}, u32[]{:S(2)}) async-start(f32[8,5,64,512]{3,2,1,0:T(8,128)} %stack.97), calls=%async_computation | async-start | bytes 10485760 | tf_op jit(solution)/shard_map/all_to_all | solution.py:71
  21.9 0.0 reduce-scatter.3.cloned.1.call-start
  22.6 0.0 copy-done.2
  22.6 0.1 bitcast_dynamic-update-slice_fusion.5
  22.7 1.9 collective-permute-start.1
  24.6 3.6 collective-permute-start
  28.3 2.1 collective-permute-done.1
  30.4 1.8 collective-permute-done
  32.1 0.1 pad_maximum_fusion
  32.2 1.3 collective-permute-start.2
  33.7 0.0 copy-done.3
  33.7 0.7 fusion.37
  36.9 0.1 stack.115
  37.0 0.1 stack.111
  37.1 4.6 %collective-permute-start.3 = (f32[64,3,1,2,512]{4,0,3,2,1:T(8,128)S(1)}, f32[64,3,1,2,512]{4,0,3,2,1:T(8,128)S(1)}, u32[]{:S(2)}, u32[]{:S(2)}) collective-permute-start(f32[64,3,1,2,512]{4,0,3,2,1:T(8,128)S(1)} %pad_maximum_fusion), channel_id=1, source_target_pairs={{0,8},{8,16},{16,24},{1,9},{9,17},{17,25},{2,10},{10,18},{18,26},{... | collective-permute-start | bytes 2359304 | tf_op jit(solution)/shard_map/ppermute | solution.py:19
  41.7 0.1 fusion.30
  41.8 111.2 %collective-permute-done.2 = f32[64,3,1,2,512]{4,0,3,2,1:T(8,128)} collective-permute-done((f32[64,3,1,2,512]{4,0,3,2,1:T(8,128)S(1)}, f32[64,3,1,2,512]{4,0,3,2,1:T(8,128)}, u32[]{:S(2)}, u32[]{:S(2)}) %collective-permute-start.2) | collective-permute-done | bytes 786464 | tf_op jit(solution)/shard_map/ppermute | solution.py:21
  153.0 1.0 fusion.27
  154.0 0.0 collective-permute-done.3
  154.0 1.1 copy-done.1
  155.1 1.8 multiply_subtract_fusion.2
  156.8 0.0 all-to-all-done
  156.8 3.1 copy.27
  159.9 0.0 copy-start
  159.9 2.3 copy-done
  162.3 5.1 %convolution_bitcast_fusion.1 = f32[512,1,1,2,512]{4,0,3,2,1:T(8,128)} fusion(f32[64,1,1,5,1,512]{5,0,3,4,2,1:T(8,128)S(1)} %get-tuple-element.17, f32[64,1,1,5,1,512]{5,0,3,4,2,1:T(8,128)S(1)} %get-tuple-element.18, f32[5,512,512]{2,1,0:T(8,128)S(1)} %bitcast.165, s32[]{:T(128)S(6)} %select_n.4), kind=kOutput, calls=%fused_computation.1 | convolution fusion | flops 2013593600 | bytes 4718596 | tf_op jit(solution)/shard_map/kic,cabkpm->iabpm/dot_general | solution.py:88
  167.3 0.0 reduce-scatter.3.cloned.1.call-update
  167.4 0.0 reduce-scatter.5.cloned.1.call-start
  167.4 0.6 copy-done.4
  168.0 0.7 fusion.38
  170.0 94.9 %reduce-scatter.3.cloned.1.call-done = f32[64,1,1,2,512]{4,0,3,2,1:T(8,128)} async-done(((f32[512,1,1,2,512]{4,0,3,2,1:T(8,128)}), f32[64,1,1,2,512]{4,0,3,2,1:T(8,128)}) %reduce-scatter.3.cloned.1.call-update) | async-done | bytes 262160 | tf_op jit(solution)/shard_map/reduce_scatter | solution.py:87
  264.9 5.5 %bitcast_dynamic-update-slice_fusion.2 = (f32[64,1,1,5,2,512]{5,0,3,4,2,1:T(8,128)S(1)}, f32[64,1,1,2,512]{4,0,3,2,1:T(8,128)S(1)}) fusion(f32[]{:T(128)} %bitcast, f32[64,1,1,2,512]{4,0,3,2,1:T(8,128)S(1)} %get-tuple-element.6, f32[]{:T(128)} %bitcast.33, f32[64,1,1,2,512]{4,0,3,2,1:T(8,128)} %reduce-scatter.3.cloned.1.call-done, ...), kind=kOutput, calls=%fused_computation.52 | convolution fusion | flops 2013855744 | bytes 7602184 | tf_op jit(solution)/shard_map/iabkpc,kcm->iabpm/dot_general | solution.py:84
  270.4 1.9 collective-permute-start.5
  272.4 3.6 collective-permute-start.4
  276.0 2.1 collective-permute-done.5
  278.1 1.8 collective-permute-done.4
  279.9 0.1 pad_maximum_fusion.1
  280.0 1.3 collective-permute-start.6
  281.3 4.8 %collective-permute-start.7 = (f32[64,3,1,2,512]{4,0,3,2,1:T(8,128)S(1)}, f32[64,3,1,2,512]{4,0,3,2,1:T(8,128)S(1)}, u32[]{:S(2)}, u32[]{:S(2)}) collective-permute-start(f32[64,3,1,2,512]{4,0,3,2,1:T(8,128)S(1)} %pad_maximum_fusion.1), channel_id=1, source_target_pairs={{0,8},{8,16},{16,24},{1,9},{9,17},{17,25},{2,10},{10,18},{18,26},{... | collective-permute-start | bytes 2359304 | tf_op jit(solution)/shard_map/ppermute | solution.py:19
  286.1 15.4 %collective-permute-done.6 = f32[64,3,1,2,512]{4,0,3,2,1:T(8,128)S(1)} collective-permute-done((f32[64,3,1,2,512]{4,0,3,2,1:T(8,128)S(1)}, f32[64,3,1,2,512]{4,0,3,2,1:T(8,128)S(1)}, u32[]{:S(2)}, u32[]{:S(2)}) %collective-permute-start.6) | collective-permute-done | bytes 786464 | tf_op jit(solution)/shard_map/ppermute | solution.py:21
  301.6 1.8 collective-permute-done.7
  303.3 0.3 multiply_subtract_fusion
  303.7 6.4 %convolution_bitcast_fusion = f32[512,1,1,2,512]{4,0,3,2,1:T(8,128)} fusion(f32[64,1,1,5,1,512]{5,0,3,4,2,1:T(8,128)S(1)} %get-tuple-element.15, f32[64,1,1,5,1,512]{5,0,3,4,2,1:T(8,128)S(1)} %get-tuple-element.16, f32[5,512,512]{2,1,0:T(8,128)} %bitcast.167, s32[]{:T(128)S(6)} %select_n.4), kind=kOutput, calls=%fused_computation | convolution fusion | flops 2013593600 | bytes 4718596 | tf_op jit(solution)/shard_map/kic,cabkpm->iabpm/dot_general | solution.py:88
  310.1 0.0 reduce-scatter.5.cloned.1.call-update
  310.1 93.4 %reduce-scatter.5.cloned.1.call-done = f32[64,1,1,2,512]{4,0,3,2,1:T(8,128)} async-done(((f32[512,1,1,2,512]{4,0,3,2,1:T(8,128)}), f32[64,1,1,2,512]{4,0,3,2,1:T(8,128)}) %reduce-scatter.5.cloned.1.call-update) | async-done | bytes 262160 | tf_op jit(solution)/shard_map/reduce_scatter | solution.py:87
  403.5 5.6 %fusion.23 = f32[64,1,1,2,512]{4,0,3,2,1:T(8,128)S(1)} fusion(f32[64,1,1,2,512]{4,0,3,2,1:T(8,128)} %reduce-scatter.5.cloned.1.call-done, f32[5,512,512,1]{2,1,0,3:T(8,128)} %bitcast.168, f32[64,1,1,5,1,512]{5,0,3,4,2,1:T(8,128)S(1)} %get-tuple-element.8, f32[64,1,1,5,1,512]{5,0,3,4,2,1:T(8,128)S(1)} %get-tuple-element.7, ...), kind=kOutput, calls=%fused_computation.29 | convolution fusion | flops 2014117888 | bytes 7602184 | tf_op jit(solution)/shard_map/iabkpc,kcm->iabpm/dot_general | solution.py:84
  409.1 0.9 copy.35
  (13 shorter events, 0.2 us)
Async XLA Ops:
  10.7 11.9 %copy-start.2 = (f32[64,1,1,2,512]{4,3,2,1,0:T(2,128)S(1)}, f32[64,1,1,2,512]{4,3,2,1,0:T(2,128)}, u32[]{:S(2)}) copy-start(f32[64,1,1,2,512]{4,3,2,1,0:T(2,128)} %param.5) | copy-start | bytes 786436
  10.7 146.2 %all-to-all-start = ((f32[8,5,64,512]{3,2,1,0:T(8,128)}), f32[8,5,64,512]{3,2,1,0:T(8,128)}, u32[]{:S(2)}, u32[]{:S(2)}) async-start(f32[8,5,64,512]{3,2,1,0:T(8,128)} %stack.97), calls=%async_computation | async-start | bytes 10485760 | tf_op jit(solution)/shard_map/all_to_all | solution.py:71
  21.9 11.8 %copy-start.3 = (f32[2,2]{1,0:T(2,128)S(1)}, f32[2,2]{1,0:T(2,128)}, u32[]{:S(2)}) copy-start(f32[2,2]{1,0:T(2,128)} %param.8) | copy-start | bytes 52
  21.9 243.0 %reduce-scatter.3.cloned.1.call-start = ((), (), s32[]{:S(2)}) async-start(), calls=%async_computation.3 | async-start | bytes 2359296 | tf_op jit(solution)/shard_map/reduce_scatter | solution.py:87
  22.7 7.7 %collective-permute-start.1 = (f32[64,1,1,2,512]{4,0,3,2,1:T(8,128)S(1)}, f32[64,1,1,2,512]{4,0,3,2,1:T(8,128)S(1)}, u32[]{:S(2)}, u32[]{:S(2)}) collective-permute-start(f32[64,1,1,2,512]{4,0,3,2,1:T(8,128)S(1)} %get-tuple-element.6), channel_id=1, source_target_pairs={{0,32},{32,64},{64,96},{96,128},{128,160},{160,192},{192,224},{1,3... | collective-permute-start | bytes 786440 | tf_op jit(solution)/shard_map/ppermute | solution.py:19
  24.6 7.5 %collective-permute-start = (f32[64,1,1,2,512]{4,0,3,2,1:T(8,128)S(1)}, f32[64,1,1,2,512]{4,0,3,2,1:T(8,128)S(1)}, u32[]{:S(2)}, u32[]{:S(2)}) collective-permute-start(f32[64,1,1,2,512]{4,0,3,2,1:T(8,128)S(1)} %get-tuple-element.6), channel_id=1, source_target_pairs={{32,0},{64,32},{96,64},{128,96},{160,128},{192,160},{224,192},{33,... | collective-permute-start | bytes 786440 | tf_op jit(solution)/shard_map/ppermute | solution.py:21
  32.2 120.8 %collective-permute-start.2 = (f32[64,3,1,2,512]{4,0,3,2,1:T(8,128)S(1)}, f32[64,3,1,2,512]{4,0,3,2,1:T(8,128)}, u32[]{:S(2)}, u32[]{:S(2)}) collective-permute-start(f32[64,3,1,2,512]{4,0,3,2,1:T(8,128)S(1)} %pad_maximum_fusion), channel_id=1, source_target_pairs={{8,0},{16,8},{24,16},{9,1},{17,9},{25,17},{10,2},{18,10},{26,18},{... | collective-permute-start | bytes 2359304 | tf_op jit(solution)/shard_map/ppermute | solution.py:21
  37.1 116.9 %collective-permute-start.3 = (f32[64,3,1,2,512]{4,0,3,2,1:T(8,128)S(1)}, f32[64,3,1,2,512]{4,0,3,2,1:T(8,128)S(1)}, u32[]{:S(2)}, u32[]{:S(2)}) collective-permute-start(f32[64,3,1,2,512]{4,0,3,2,1:T(8,128)S(1)} %pad_maximum_fusion), channel_id=1, source_target_pairs={{0,8},{8,16},{16,24},{1,9},{9,17},{17,25},{2,10},{10,18},{18,26},{... | collective-permute-start | bytes 2359304 | tf_op jit(solution)/shard_map/ppermute | solution.py:19
  154.0 1.1 copy-start.1
  159.9 2.3 copy-start
  167.3 0.7 copy-start.4
  167.4 236.2 %reduce-scatter.5.cloned.1.call-start = ((), (), s32[]{:S(2)}) async-start(), calls=%async_computation.4 | async-start | bytes 2359296 | tf_op jit(solution)/shard_map/reduce_scatter | solution.py:87
  270.4 7.7 %collective-permute-start.5 = (f32[64,1,1,2,512]{4,0,3,2,1:T(8,128)S(1)}, f32[64,1,1,2,512]{4,0,3,2,1:T(8,128)S(1)}, u32[]{:S(2)}, u32[]{:S(2)}) collective-permute-start(f32[64,1,1,2,512]{4,0,3,2,1:T(8,128)S(1)} %get-tuple-element.26), channel_id=1, source_target_pairs={{0,32},{32,64},{64,96},{96,128},{128,160},{160,192},{192,224},{1,3... | collective-permute-start | bytes 786440 | tf_op jit(solution)/shard_map/ppermute | solution.py:19
  272.4 7.5 %collective-permute-start.4 = (f32[64,1,1,2,512]{4,0,3,2,1:T(8,128)S(1)}, f32[64,1,1,2,512]{4,0,3,2,1:T(8,128)S(1)}, u32[]{:S(2)}, u32[]{:S(2)}) collective-permute-start(f32[64,1,1,2,512]{4,0,3,2,1:T(8,128)S(1)} %get-tuple-element.26), channel_id=1, source_target_pairs={{32,0},{64,32},{96,64},{128,96},{160,128},{192,160},{224,192},{33,... | collective-permute-start | bytes 786440 | tf_op jit(solution)/shard_map/ppermute | solution.py:21
  280.0 21.6 %collective-permute-start.6 = (f32[64,3,1,2,512]{4,0,3,2,1:T(8,128)S(1)}, f32[64,3,1,2,512]{4,0,3,2,1:T(8,128)S(1)}, u32[]{:S(2)}, u32[]{:S(2)}) collective-permute-start(f32[64,3,1,2,512]{4,0,3,2,1:T(8,128)S(1)} %pad_maximum_fusion.1), channel_id=1, source_target_pairs={{8,0},{16,8},{24,16},{9,1},{17,9},{25,17},{10,2},{18,10},{26,18},{... | collective-permute-start | bytes 2359304 | tf_op jit(solution)/shard_map/ppermute | solution.py:21
  281.3 22.0 %collective-permute-start.7 = (f32[64,3,1,2,512]{4,0,3,2,1:T(8,128)S(1)}, f32[64,3,1,2,512]{4,0,3,2,1:T(8,128)S(1)}, u32[]{:S(2)}, u32[]{:S(2)}) collective-permute-start(f32[64,3,1,2,512]{4,0,3,2,1:T(8,128)S(1)} %pad_maximum_fusion.1), channel_id=1, source_target_pairs={{0,8},{8,16},{16,24},{1,9},{9,17},{17,25},{2,10},{10,18},{18,26},{... | collective-permute-start | bytes 2359304 | tf_op jit(solution)/shard_map/ppermute | solution.py:19
Sparse Core Ops, SparseCore 0:
  167.5 97.3 reduce-scatter.2
  310.2 93.2 reduce-scatter.4
